TPU v7x, 32 devices: a whole 2x2x4 slice. The times are simulated.
32 devices in a mesh: parts: 2 (over y), tile: 4 (over x, core), chan: 4 (over z).
Axes of the slice: x: 2, y: 2, z: 4, core: 2. Of those that a mesh axis runs over, the one named last changes fastest.
Arguments:
- weather: bfloat16 [768, 64, 1440], P('chan', 'parts', 'tile'), parts along dimension 1, may hold values from -6 to 6
- lon_taps: float32 [9, 768], P(None, 'chan'), may hold values from -4 to 4
- latitude_taps: float32 [9, 768], P(None, 'chan'), may hold values from -2 to 2
- norm_gain: float32 [768], replicated, may hold values from 0.1 to 1.9
- up_weight: bfloat16 [768, 3072], P(None, ('tile', 'chan')), may hold values from -0.21875 to 0.21875
- down_weight: bfloat16 [768, 3072], P(None, ('tile', 'chan')), may hold values from -0.109375 to 0.109375
Outputs:
- mixed: bfloat16 [768, 64, 1440], P('chan', 'parts', 'tile'), parts along dimension 1
There are 2 independent parts, one for each index of `parts`. A program takes and returns all parts, laid end to end along the dimension named above; an argument that names none is the same for every part. Nothing has to cross between parts.
All inputs are finite; a program needn't handle non-finite values.
Results may differ from a plain program's by a relative error of at most 0.0065.
Values may be sent and summed in bfloat16 or wider, within the bound.
No kernel may reach another device: no remote copies, remote signals or barrier semaphores. Data moves between devices by JAX's collectives and lax.ppermute only.
A program may use at most 128 MiB of HBM per device.

v0:
```python
import jax
import jax.numpy as jnp
from jax import lax
from jax.sharding import PartitionSpec as P

KERNEL_TAPS = 9
DILATION_STEP = 2


def with_halo(shard, sides, width):
    for axis, dim in sides:
        devices, length = (lax.axis_size(axis), shard.shape[dim])
        up = [(i, (i + 1) % devices) for i in range(devices)]
        down = [(j, i) for i, j in up]
        last = lax.slice_in_dim(shard, length - width, length, axis=dim)
        initial = lax.slice_in_dim(shard, 0, width, axis=dim)
        before = lax.ppermute(last, axis, up)
        after = lax.ppermute(initial, axis, down)
        shard = jnp.concatenate([before, shard, after], axis=dim)
    return shard


def layer_norm(values, norm_gain):
    as_float = values.astype(jnp.float32)
    center = jnp.mean(as_float, axis=0)
    deviation = as_float - center
    spread_sq = jnp.mean(deviation * deviation, axis=0)
    return (deviation * lax.rsqrt(spread_sq + 1e-06) * norm_gain[:, None]).astype(jnp.bfloat16)


def on_device(weather, lon_taps, latitude_taps, norm_gain, up_weight, down_weight):
    chan_count, row_total, column_total = weather.shape
    border_width = DILATION_STEP * (KERNEL_TAPS // 2)
    widened_field = with_halo(weather, (("tile", 2),), border_width)
    lon_sum = jnp.zeros(weather.shape, jnp.float32)
    for kernel_tap_index in range(KERNEL_TAPS):
        sliding_window = widened_field[
            :, :, DILATION_STEP * kernel_tap_index : DILATION_STEP * kernel_tap_index + column_total
        ].astype(jnp.float32)
        lon_sum = lon_sum + lon_taps[kernel_tap_index][:, None, None] * sliding_window
    padded_field = jnp.pad(lon_sum, ((0, 0), (border_width, border_width), (0, 0)))
    latitude_sum = jnp.zeros(weather.shape, jnp.float32)
    for kernel_tap_index in range(KERNEL_TAPS):
        latitude_sum = (
            latitude_sum
            + latitude_taps[kernel_tap_index][:, None, None]
            * padded_field[
                :,
                DILATION_STEP * kernel_tap_index : DILATION_STEP * kernel_tap_index + row_total,
                :,
            ]
        )
    spatial = latitude_sum.astype(jnp.bfloat16)
    group_count = lax.axis_size("chan")
    width_all = chan_count * group_count
    shard_width = up_weight.shape[1]
    by_cell = lax.all_to_all(spatial, "chan", split_axis=1, concat_axis=0, tiled=True)
    cell_count = by_cell.shape[1] * by_cell.shape[2]
    normed = layer_norm(by_cell.reshape(width_all, cell_count), norm_gain)
    expanded = lax.dot_general(
        lax.all_gather(up_weight, ("tile", "chan"), axis=1, tiled=True),
        normed,
        (((0,), (0,)), ((), ())),
        preferred_element_type=jnp.float32,
    )
    hidden = jax.nn.gelu(expanded, approximate=False).astype(jnp.bfloat16)
    down_all = lax.all_gather(down_weight, ("tile", "chan"), axis=1, tiled=True)
    tile_count = down_all.shape[1] // (group_count * shard_width)
    down_groups = down_all.reshape(width_all, tile_count, group_count, shard_width)
    hidden_groups = hidden.reshape(tile_count, group_count, shard_width, cell_count)
    summed = jnp.zeros((width_all, cell_count), jnp.float32)
    for group in range(group_count):
        group_value = jnp.einsum(
            "dts,tsc->dc",
            down_groups[:, :, group, :],
            hidden_groups[:, group],
            preferred_element_type=jnp.float32,
        ).astype(jnp.bfloat16)
        group_value = lax.optimization_barrier(group_value)
        summed = summed + group_value.astype(jnp.float32)
    update_cells = summed.astype(jnp.bfloat16).reshape(width_all, by_cell.shape[1], column_total)
    update = lax.all_to_all(update_cells, "chan", split_axis=0, concat_axis=1, tiled=True)
    return (weather.astype(jnp.float32) + update.astype(jnp.float32)).astype(jnp.bfloat16)


def solution(mesh):
    return jax.shard_map(
        on_device,
        mesh=mesh,
        in_specs=(
            P("chan", "parts", "tile"),
            P(None, "chan"),
            P(None, "chan"),
            P(),
            P(None, ("tile", "chan")),
            P(None, ("tile", "chan")),
        ),
        out_specs=P("chan", "parts", "tile"),
        check_vma=False,
    )
```

profile of v0, /device:TPU:0, one launch (start us, length us, event | category | flops | bytes accessed | tf_op | source)
XLA Modules:
  0.0 563.3 jit_solution(12894988400171444290)
XLA Ops:
  6.5 0.0 copy-start.1
  6.5 0.0 copy-start.2
  6.5 0.0 all-gather.3.cloned.1.call-start
  6.5 0.7 all-gather.3.cloned.1.call-update
  7.3 2.6 fusion.56
  9.9 1.3 copy.53
  11.2 2.4 collective-permute-start.1
  13.6 1.3 copy.52
  14.9 0.1 collective-permute-start
  14.9 0.0 copy-done.1
  14.9 0.0 copy-done.2
  15.0 4.3 collective-permute-done
  19.3 1.3 copy.36
  20.6 0.0 collective-permute-done.1
  20.6 1.3 copy.38
  22.0 36.4 %fusion.22 = f32[192,32,360]{2,1,0:T(8,128)} fusion(bf16[192,32,360]{2,1,0:T(8,128)(2,1)} %param.6, bf16[192,32,8]{2,1,0:T(8,128)(2,1)S(1)} %copy.38, bf16[192,32,8]{2,1,0:T(8,128)(2,1)S(1)} %copy.36, f32[192]{0:T(256)S(1)} %bitcast.205, f32[192]{0:T(256)S(1)} %bitcast.206, f32[192]{0:T(256)S(1)} %bitcast.199, f32[192]{0:T(256)S(1)} %bitcast.200, ...), kind=kLoop, calls=%fused_computation.38 | loop fusion | flops 110592000 | bytes 13474560 | tf_op jit(solution)/shard_map/add | solution.py:40
  58.4 34.3 %fusion.33 = bf16[192,32,360]{2,1,0:T(8,128)(2,1)S(1)} fusion(f32[192,32,360]{2,1,0:T(8,128)} %fusion.22, f32[192]{0:T(256)S(1)} %bitcast.196, f32[192]{0:T(256)S(1)} %bitcast.197, f32[192]{0:T(256)S(1)} %bitcast.190, f32[192]{0:T(256)S(1)} %bitcast.191, f32[192]{0:T(256)S(1)} %bitcast.192, f32[192]{0:T(256)S(1)} %bitcast.193, f32[192]{0:T(256)S(1)} %bitcast.194, ...), kind=kLoop, calls=%fused_computation.49 | loop fusion | flops 39813120 | bytes 13277952 | tf_op jit(solution)/shard_map/convert_element_type | solution.py:53
  92.7 4.0 copy.39
  96.7 5.0 all-to-all-start
  101.6 0.3 all-gather.5.cloned.1.call-start
  101.9 0.4 all-gather.5.cloned.1.call-update
  102.4 130.9 %all-to-all-done = bf16[192,32,360]{2,0,1:T(8,128)(2,1)} async-done(((bf16[192,32,360]{2,0,1:T(8,128)(2,1)}), bf16[192,32,360]{2,0,1:T(8,128)(2,1)}, u32[]{:S(2)}, u32[]{:S(2)}) %all-to-all-start) | async-done | bytes 4423712 | tf_op jit(solution)/shard_map/all_to_all | solution.py:57
  233.2 3.5 bitcast_convert_fusion.4
  236.7 5.0 fusion.55
  241.7 9.1 %copy.68 = f32[192,4,8,360]{3,2,0,1:T(8,128)} copy(f32[192,4,8,360]{3,0,2,1:T(8,128)S(1)} %bitcast_convert_fusion.4) | data formatting | bytes 17694720 | tf_op jit(solution)/shard_map/convert_element_type | solution.py:24
  250.8 5.0 multiply_reduce_fusion
  255.8 0.0 copy-start.3
  255.9 0.1 div.9
  255.9 11.5 %reshape.71 = f32[768,2880]{1,0:T(8,128)} reshape(f32[4,192,8,360]{3,2,1,0:T(8,128)} %bitcast.180) | data formatting | bytes 17694720 | tf_op jit(solution)/shard_map/convert_element_type | solution.py:24
  267.4 0.1 rsqrt.11
  267.5 0.0 copy-done.3
  267.5 7.2 %multiply_convert_fusion.1.clone.4 = bf16[768,2880]{1,0:T(8,128)(2,1)} fusion(f32[768,2880]{1,0:T(8,128)} %reshape.71, f32[768]{0:T(1024)S(1)} %copy-done.3, f32[2880]{0:T(1024)S(1)} %rsqrt.11, f32[2880]{0:T(1024)S(1)} %div.9), kind=kLoop, calls=%fused_computation.60.clone.clone.clone.clone.1 | loop fusion | flops 8847360 | bytes 13297152 | tf_op jit(solution)/shard_map/convert_element_type | solution.py:66
  274.7 0.0 all-gather.3.cloned.1.call-done
  274.7 102.8 %fusion.2 = bf16[3072,2880]{0,1:T(8,128)(2,1)} fusion(bf16[768,3072]{0,1:T(8,128)(2,1)} %all-gather.3.cloned.1.call-done, bf16[768,2880]{1,0:T(8,128)(2,1)} %multiply_convert_fusion.1.clone.4), kind=kOutput, calls=%fused_computation.3 | convolution fusion | flops 14164623360 | bytes 26836992 | tf_op jit(solution)/shard_map/dot_general | solution.py:60
  377.5 22.1 %copy.41 = bf16[3072,2880]{1,0:T(8,128)(2,1)} copy(bf16[3072,2880]{0,1:T(8,128)(2,1)} %fusion.2) | data formatting | bytes 35389440 | tf_op jit(solution)/shard_map/convert_element_type | solution.py:66
  399.7 0.0 all-gather.5.cloned.1.call-done
  399.7 0.0 copy-start
  399.7 0.0 copy-start.4
  399.7 8.7 %fusion.53 = bf16[768,2880]{0,1:T(8,128)(2,1)} fusion(bf16[4,4,192,2880]{3,2,1,0:T(8,128)(2,1)} %bitcast.184, bf16[768,4,4,192]{0,3,2,1:T(8,128)(2,1)} %bitcast.207), kind=kOutput, calls=%fused_computation.92 | convolution fusion | flops 3399598080 | bytes 10125312 | tf_op jit(solution)/shard_map/dts,tsc->dc/dot_general | solution.py:73
  408.4 0.1 copy-done
  408.5 1.9 copy-done.4
  410.5 5.5 fusion.52
  415.9 5.6 fusion.51
  421.5 5.7 %fusion.54 = bf16[768,2880]{0,1:T(8,128)(2,1)} fusion(bf16[4,4,192,2880]{3,2,1,0:T(8,128)(2,1)S(1)} %bitcast.187, bf16[768,4,4,192]{0,3,2,1:T(8,128)(2,1)S(1)} %bitcast.210), kind=kOutput, calls=%fused_computation.93 | convolution fusion | flops 3399598080 | bytes 10125312 | tf_op jit(solution)/shard_map/dts,tsc->dc/dot_general | solution.py:73
  427.2 10.3 %add_convert_fusion = bf16[768,2880]{0,1:T(8,128)(2,1)} fusion(bf16[768,2880]{0,1:T(8,128)(2,1)} %fusion.54, bf16[768,2880]{0,1:T(8,128)(2,1)} %fusion.53, bf16[768,2880]{0,1:T(8,128)(2,1)} %fusion.52, bf16[768,2880]{0,1:T(8,128)(2,1)} %fusion.51), kind=kLoop, calls=%fused_computation.65 | loop fusion | flops 17694720 | bytes 22118400 | tf_op jit(solution)/shard_map/convert_element_type | solution.py:81
  437.6 0.0 slice-start
  437.6 7.0 %copy.50 = bf16[768,8,360]{2,1,0:T(8,128)(2,1)} copy(bf16[768,8,360]{0,2,1:T(8,128)(2,1)} %bitcast.188) | data formatting | bytes 8847360 | tf_op jit(solution)/shard_map/reshape | solution.py:81
  444.5 0.0 slice-start.1
  444.5 108.1 %all_to_all.8 = bf16[768,8,360]{2,1,0:T(8,128)(2,1)S(1)} all-to-all(bf16[768,8,360]{2,1,0:T(8,128)(2,1)} %copy.50), channel_id=1, replica_groups=mesh['parts'=2,'tile'=4,'chan'=4] {'chan'}, dimensions={0} | all-to-all | bytes 8847360 | tf_op jit(solution)/shard_map/all_to_all | solution.py:82
  552.7 0.0 slice-done
  552.7 0.0 slice-done.1
  552.7 3.4 fusion.23
  (5 shorter events, 0.0 us)
Async XLA Ops:
  6.5 8.4 %copy-start.1 = (f32[9,192]{1,0:T(8,128)S(1)}, f32[9,192]{1,0:T(8,128)}, u32[]{:S(2)}) copy-start(f32[9,192]{1,0:T(8,128)} %param.7) | copy-start | bytes 20740
  6.5 8.4 %copy-start.2 = (f32[9,192]{1,0:T(8,128)S(1)}, f32[9,192]{1,0:T(8,128)}, u32[]{:S(2)}) copy-start(f32[9,192]{1,0:T(8,128)} %param.8) | copy-start | bytes 20740
  6.5 268.1 %all-gather.3.cloned.1.call-start = ((), (), s32[]{:S(2)}) async-start(), calls=%async_computation.2 | async-start | bytes 5013504 | tf_op jit(solution)/shard_map/all_gather | solution.py:61
  11.2 9.5 %collective-permute-start.1 = (bf16[192,32,8]{0,2,1:T(8,128)(2,1)S(1)}, bf16[192,32,8]{0,2,1:T(8,128)(2,1)S(1)}, u32[]{:S(2)}, u32[]{:S(2)}) collective-permute-start(bf16[192,32,8]{0,2,1:T(8,128)(2,1)S(1)} %copy.53), channel_id=1, source_target_pairs={{4,0},{8,4},{12,8},{0,12},{5,1},{9,5},{13,9},{1,13},{6,2},{10,6},{... | collective-permute-start | bytes 294920 | tf_op jit(solution)/shard_map/ppermute | solution.py:18
  14.9 4.4 collective-permute-start
  96.7 136.6 %all-to-all-start = ((bf16[192,32,360]{2,0,1:T(8,128)(2,1)}), bf16[192,32,360]{2,0,1:T(8,128)(2,1)}, u32[]{:S(2)}, u32[]{:S(2)}) async-start(bf16[192,32,360]{2,0,1:T(8,128)(2,1)} %copy.39), calls=%async_computation | async-start | bytes 9437184 | tf_op jit(solution)/shard_map/all_to_all | solution.py:57
  101.6 298.0 %all-gather.5.cloned.1.call-start = ((), (), s32[]{:S(2)}) async-start(), calls=%async_computation.3 | async-start | bytes 5013504 | tf_op jit(solution)/shard_map/all_gather | solution.py:67
  255.8 11.7 %copy-start.3 = (f32[768]{0:T(1024)S(1)}, f32[768]{0:T(1024)}, u32[]{:S(2)}) copy-start(f32[768]{0:T(1024)} %param.9) | copy-start | bytes 9220
  399.7 8.8 %copy-start = (bf16[3072,2880]{1,0:T(8,128)(2,1)S(1)}, bf16[3072,2880]{1,0:T(8,128)(2,1)}, u32[]{:S(2)}) copy-start(bf16[3072,2880]{1,0:T(8,128)(2,1)} %copy.41) | copy-start | bytes 53084164
  399.7 10.8 %copy-start.4 = (bf16[768,3072]{0,1:T(8,128)(2,1)S(1)}, bf16[768,3072]{0,1:T(8,128)(2,1)}, u32[]{:S(2)}) copy-start(bf16[768,3072]{0,1:T(8,128)(2,1)} %all-gather.5.cloned.1.call-done) | copy-start | bytes 14155780
  437.6 115.1 %slice-start = ((s8[4718592]{0:T(1024)(128)(4,1)}), s8[524288]{0:T(1024)(128)(4,1)S(1)}, s32[]{:S(2)}) async-start(s8[4718592]{0:T(1024)(128)(4,1)} %bitcast.181), calls=%async_computation.4 | async-start | bytes 1048576
  444.5 108.1 %slice-start.1 = ((s8[4718592]{0:T(1024)(128)(4,1)}), s8[4194304]{0:T(1024)(128)(4,1)S(1)}, s32[]{:S(2)}) async-start(s8[4718592]{0:T(1024)(128)(4,1)} %bitcast.181), calls=%async_computation.5 | async-start | bytes 8388608
Sparse Core Ops, SparseCore 0:
  9.7 56.0 all-gather.2
  104.8 103.3 all-gather.4
where the time goes:
time: 572 us; the launch traced here: 563 us
  waiting for transfers between devices  136 us (24%)
  matrix products  128 us (22%)
  blocking collectives  108 us (19%)
  other arithmetic  105 us (18%)
  local copies, waits for them, and re-layouts  63.8 us (11%)
  between operations  14 us (2%)
  starting transfers between devices  7.74 us (1%)
    all_to_all x1, waiting for transfers between devices, on_device(): lax.all_to_all(spatial, 'chan', split_axis=1, concat_axis=0, tiled=True)  131 us
    all_to_all x1, blocking collectives, on_device(): lax.all_to_all(update_cells, 'chan', split_axis=0, concat_axis=1, tiled=T...  108 us
    dot_general x1, matrix products, on_device(): lax.dot_general(lax.all_gather(up_weight, ('tile', 'chan'), axis=1, tiled...  103 us
    add x1, other arithmetic, on_device(): lon_sum + lon_taps[kernel_tap_index][:, None, None] * sliding_window  36.4 us
    convert_element_type x1, other arithmetic, on_device(): spatial = latitude_sum.astype(jnp.bfloat16)  34.3 us
    dot_general x4, matrix products, on_device(): jnp.einsum('dts,tsc->dc', down_groups[:, :, group, :], hidden_groups[:, g...  25.5 us
    convert_element_type x1, local copies, waits for them, and re-layouts, on_device(): hidden = jax.nn.gelu(expanded, approximate=False).astype(jnp.bfloat16)  22.1 us
    convert_element_type x2, local copies, waits for them, and re-layouts, layer_norm(): as_float = values.astype(jnp.float32)  20.6 us
  transfers between devices with their start and end apart: 5, of which 2 were waited for; matrix products, arithmetic and copies ran while one was open for 44% of the time, Pallas kernels for 0%

commit v1 on v0

--- a/solution.py
+++ b/solution.py
@@ -79,7 +79,18 @@
         group_value = lax.optimization_barrier(group_value)
         summed = summed + group_value.astype(jnp.float32)
     update_cells = summed.astype(jnp.bfloat16).reshape(width_all, by_cell.shape[1], column_total)
-    update = lax.all_to_all(update_cells, "chan", split_axis=0, concat_axis=1, tiled=True)
+    ways, here = (lax.axis_size("chan"), lax.axis_index("chan"))
+    width_2 = update_cells.shape[0] // ways
+    lengths = list(update_cells.shape)
+    lengths[0] = width_2
+    height = lengths[1]
+    lengths[1] = height * ways
+    update = jnp.zeros(lengths, update_cells.dtype)
+    for mask in range(ways):
+        part = lax.dynamic_slice_in_dim(update_cells, (here ^ mask) * width_2, width_2, axis=0)
+        if mask:
+            part = lax.ppermute(part, "chan", [(d, d ^ mask) for d in range(ways)])
+        update = lax.dynamic_update_slice_in_dim(update, part, (here ^ mask) * height, axis=1)
     return (weather.astype(jnp.float32) + update.astype(jnp.float32)).astype(jnp.bfloat16)
 
 

time: 572 us -> 545 us (0.953)
  the two profiles are of different devices: /device:TPU:0 before, /device:TPU:8 now
where the time goes in v1:
time: 545 us; the launch traced here: 535 us
  waiting for transfers between devices  211 us (39%)
  matrix products  118 us (22%)
  local copies, waits for them, and re-layouts  90.3 us (17%)
  other arithmetic  76.7 us (14%)
  starting transfers between devices  25.1 us (5%)
  between operations  13.9 us (3%)
    all_to_all x1, waiting for transfers between devices, on_device(): lax.all_to_all(spatial, 'chan', split_axis=1, concat_axis=0, tiled=True)  117 us
    ppermute x3, waiting for transfers between devices, on_device(): part = lax.ppermute(part, 'chan', [(d, d ^ mask) for d in range(ways)])  94.6 us
    dot_general x1, matrix products, on_device(): lax.dot_general(lax.all_gather(up_weight, ('tile', 'chan'), axis=1, tiled...  92.7 us
    add x1, other arithmetic, on_device(): lon_sum + lon_taps[kernel_tap_index][:, None, None] * sliding_window  32.8 us
    dot_general x4, matrix products, on_device(): jnp.einsum('dts,tsc->dc', down_groups[:, :, group, :], hidden_groups[:, g...  25.4 us
    convert_element_type x2, local copies, waits for them, and re-layouts, layer_norm(): as_float = values.astype(jnp.float32)  24.3 us
    convert_element_type x1, local copies, waits for them, and re-layouts, on_device(): hidden = jax.nn.gelu(expanded, approximate=False).astype(jnp.bfloat16)  22.3 us
    unnamed x23, local copies, waits for them, and re-layouts  18.5 us
  transfers between devices with their start and end apart: 8, of which 4 were waited for; matrix products, arithmetic and copies ran while one was open for 42% of the time, Pallas kernels for 0%

profile of v1, /device:TPU:8, one launch (start us, length us, event | category | flops | bytes accessed | tf_op | source)
XLA Modules:
  0.0 535.4 jit_solution(8554043133220136035)
XLA Ops:
  6.5 0.0 copy-start.2
  6.5 0.0 all-gather.3.cloned.1.call-start
  6.5 2.6 fusion.56
  9.1 1.3 copy.51
  10.4 0.1 collective-permute-start
  10.5 1.3 copy.52
  11.8 1.8 collective-permute-start.1
  13.6 0.0 all-gather.3.cloned.1.call-update
  13.6 0.0 copy-done.2
  13.6 0.6 fusion.58
  14.2 1.0 fusion.57
  15.2 6.2 %copy.29 = bf16[192,32,360]{2,0,1:T(8,128)(2,1)} copy(bf16[192,32,360]{2,1,0:T(8,128)(2,1)} %param.6) | data formatting | bytes 8847360 | tf_op args[0]
  21.4 0.0 collective-permute-done
  21.4 0.8 copy.31
  22.2 0.0 collective-permute-done.1
  22.2 1.5 copy.35
  23.8 0.0 copy-done.4
  23.8 32.8 %fusion.22 = f32[192,32,360]{2,0,1:T(8,128)S(1)} fusion(bf16[192,32,360]{2,0,1:T(8,128)(2,1)} %copy.29, bf16[192,32,8]{2,0,1:T(8,128)(2,1)} %copy.35, bf16[192,32,8]{2,0,1:T(8,128)(2,1)S(1)} %copy.31, f32[192]{0:T(256)S(1)} %bitcast.197, f32[192]{0:T(256)S(1)} %bitcast.198, f32[192]{0:T(256)S(1)} %bitcast.191, f32[192]{0:T(256)S(1)} %bitcast.192, ...), kind=kLoop, calls=%fused_computation.38 | loop fusion | flops 110592000 | bytes 13474560 | tf_op jit(solution)/shard_map/add | solution.py:40
  56.6 10.9 %fusion.33 = bf16[192,32,360]{2,0,1:T(8,128)(2,1)} fusion(f32[192,32,360]{2,0,1:T(8,128)S(1)} %fusion.22, f32[192]{0:T(256)S(1)} %bitcast.188, f32[192]{0:T(256)S(1)} %bitcast.189, f32[192]{0:T(256)S(1)} %bitcast.182, f32[192]{0:T(256)S(1)} %bitcast.183, f32[192]{0:T(256)S(1)} %bitcast.184, f32[192]{0:T(256)S(1)} %bitcast.185, f32[192]{0:T(256)S(1)} %bitcast.186, ...), kind=kLoop, calls=%fused_computation.49 | loop fusion | flops 39813120 | bytes 13277952 | tf_op jit(solution)/shard_map/convert_element_type | solution.py:53
  67.5 5.3 all-to-all-start
  72.8 13.1 %all-gather.5.cloned.1.call-start = ((), (), s32[]{:S(2)}) async-start(), calls=%async_computation.2 | async-start | bytes 5013504 | tf_op jit(solution)/shard_map/all_gather | solution.py:67
  85.9 0.0 all-gather.5.cloned.1.call-update
  85.9 116.8 %all-to-all-done = bf16[192,32,360]{2,0,1:T(8,128)(2,1)} async-done(((bf16[192,32,360]{2,0,1:T(8,128)(2,1)}), bf16[192,32,360]{2,0,1:T(8,128)(2,1)}, u32[]{:S(2)}, u32[]{:S(2)}) %all-to-all-start) | async-done | bytes 4423712 | tf_op jit(solution)/shard_map/all_to_all | solution.py:57
  202.7 3.5 bitcast_convert_fusion.4
  206.2 0.0 copy-start
  206.3 5.0 fusion.55
  211.2 0.0 copy-done
  211.3 5.0 multiply_reduce_fusion
  216.3 0.1 div.9
  216.4 12.8 %copy.71 = f32[192,4,8,360]{3,2,0,1:T(8,128)} copy(f32[192,4,8,360]{3,0,2,1:T(8,128)} %copy-done) | data formatting | bytes 17694720 | tf_op jit(solution)/shard_map/convert_element_type | solution.py:24
  229.2 0.1 rsqrt.11
  229.3 11.5 %reshape.67 = f32[768,2880]{1,0:T(8,128)} reshape(f32[4,192,8,360]{3,2,1,0:T(8,128)} %bitcast.173) | data formatting | bytes 17694720 | tf_op jit(solution)/shard_map/convert_element_type | solution.py:24
  240.8 0.0 copy-done.3
  240.8 7.1 %multiply_convert_fusion.1.clone.4 = bf16[768,2880]{1,0:T(8,128)(2,1)} fusion(f32[768,2880]{1,0:T(8,128)} %reshape.67, f32[768]{0:T(1024)S(1)} %copy-done.3, f32[2880]{0:T(1024)S(1)} %rsqrt.11, f32[2880]{0:T(1024)S(1)} %div.9), kind=kLoop, calls=%fused_computation.59.clone.clone.clone.clone.1 | loop fusion | flops 8847360 | bytes 13297152 | tf_op jit(solution)/shard_map/convert_element_type | solution.py:66
  247.9 92.7 %fusion.2 = bf16[3072,2880]{0,1:T(8,128)(2,1)} fusion(bf16[768,3072]{0,1:T(8,128)(2,1)} %all-gather.3.cloned.1.call-done, bf16[768,2880]{1,0:T(8,128)(2,1)} %multiply_convert_fusion.1.clone.4), kind=kOutput, calls=%fused_computation.3 | convolution fusion | flops 14164623360 | bytes 26836992 | tf_op jit(solution)/shard_map/dot_general | solution.py:60
  340.6 22.3 %copy.37 = bf16[3072,2880]{1,0:T(8,128)(2,1)} copy(bf16[3072,2880]{0,1:T(8,128)(2,1)} %fusion.2) | data formatting | bytes 35389440 | tf_op jit(solution)/shard_map/convert_element_type | solution.py:66
  362.8 8.7 %fusion.51 = bf16[768,2880]{0,1:T(8,128)(2,1)} fusion(bf16[4,4,192,2880]{3,2,1,0:T(8,128)(2,1)} %bitcast.177, bf16[768,4,4,192]{0,3,2,1:T(8,128)(2,1)} %bitcast.199), kind=kOutput, calls=%fused_computation.89 | convolution fusion | flops 3399598080 | bytes 10125312 | tf_op jit(solution)/shard_map/dts,tsc->dc/dot_general | solution.py:73
  371.5 0.1 copy-done.1
  371.7 1.9 copy-done.5
  373.6 5.5 %fusion.52 = bf16[768,2880]{0,1:T(8,128)(2,1)} fusion(bf16[4,4,192,2880]{3,2,1,0:T(8,128)(2,1)S(1)} %bitcast.178, bf16[768,4,4,192]{0,3,2,1:T(8,128)(2,1)S(1)} %bitcast.200), kind=kOutput, calls=%fused_computation.90 | convolution fusion | flops 3399598080 | bytes 10125312 | tf_op jit(solution)/shard_map/dts,tsc->dc/dot_general | solution.py:73
  379.2 5.5 %fusion.53 = bf16[768,2880]{0,1:T(8,128)(2,1)} fusion(bf16[4,4,192,2880]{3,2,1,0:T(8,128)(2,1)S(1)} %bitcast.179, bf16[768,4,4,192]{0,3,2,1:T(8,128)(2,1)S(1)} %bitcast.201), kind=kOutput, calls=%fused_computation.91 | convolution fusion | flops 3399598080 | bytes 10125312 | tf_op jit(solution)/shard_map/dts,tsc->dc/dot_general | solution.py:73
  384.6 5.7 %fusion.54 = bf16[768,2880]{0,1:T(8,128)(2,1)} fusion(bf16[4,4,192,2880]{3,2,1,0:T(8,128)(2,1)S(1)} %bitcast.180, bf16[768,4,4,192]{0,3,2,1:T(8,128)(2,1)S(1)} %bitcast.202), kind=kOutput, calls=%fused_computation.92 | convolution fusion | flops 3399598080 | bytes 10125312 | tf_op jit(solution)/shard_map/dts,tsc->dc/dot_general | solution.py:73
  390.3 10.3 %add_convert_fusion = bf16[768,2880]{0,1:T(8,128)(2,1)} fusion(bf16[768,2880]{0,1:T(8,128)(2,1)} %fusion.54, bf16[768,2880]{0,1:T(8,128)(2,1)} %fusion.53, bf16[768,2880]{0,1:T(8,128)(2,1)} %fusion.52, bf16[768,2880]{0,1:T(8,128)(2,1)} %fusion.51), kind=kLoop, calls=%fused_computation.64 | loop fusion | flops 17694720 | bytes 22118400 | tf_op jit(solution)/shard_map/convert_element_type | solution.py:81
  400.7 8.0 %constant_dynamic-slice_fusion = (bf16[192,8,360]{0,2,1:T(8,128)(2,1)S(1)}, bf16[192,8,360]{0,2,1:T(8,128)(2,1)}, bf16[192,8,360]{0,2,1:T(8,128)(2,1)}, bf16[192,8,360]{0,2,1:T(8,128)(2,1)S(1)}) fusion(bf16[768,8,360]{0,2,1:T(8,128)(2,1)} %bitcast.176, s32[]{:T(128)S(6)} %select_n.30, s32[]{:T(128)S(6)} %select_n.28, s32[]{:T(128)S(6)} %select_n.26, ...), kind=kLoop, calls=%fused_computation.100 | loop fusion | bytes 8847376 | tf_op jit(solution)/shard_map/dynamic_slice | solution.py:90
  408.7 2.5 copy.62
  411.2 3.4 collective-permute-start.2
  414.6 2.5 copy.63
  417.1 0.1 collective-permute-start.3
  417.2 1.5 copy.64
  418.7 1.4 collective-permute-start.4
  420.1 1.1 copy.61
  421.2 0.0 slice-start.1
  421.2 0.7 broadcast_in_dim.2
  421.9 0.2 constant_dynamic-update-slice_fusion.3
  422.2 38.8 %collective-permute-done.2 = bf16[192,8,360]{2,0,1:T(8,128)(2,1)} collective-permute-done((bf16[192,8,360]{2,0,1:T(8,128)(2,1)}, bf16[192,8,360]{2,0,1:T(8,128)(2,1)}, u32[]{:S(2)}, u32[]{:S(2)}) %collective-permute-start.2) | collective-permute-done | bytes 1105952 | tf_op jit(solution)/shard_map/ppermute | solution.py:92
  461.0 1.5 constant_dynamic-update-slice_fusion.2
  462.5 32.0 %collective-permute-done.3 = bf16[192,8,360]{2,0,1:T(8,128)(2,1)} collective-permute-done((bf16[192,8,360]{2,0,1:T(8,128)(2,1)}, bf16[192,8,360]{2,0,1:T(8,128)(2,1)}, u32[]{:S(2)}, u32[]{:S(2)}) %collective-permute-start.3) | collective-permute-done | bytes 1105952 | tf_op jit(solution)/shard_map/ppermute | solution.py:92
  494.5 1.5 constant_dynamic-update-slice_fusion.1
  496.0 23.7 %collective-permute-done.4 = bf16[192,8,360]{2,0,1:T(8,128)(2,1)} collective-permute-done((bf16[192,8,360]{2,0,1:T(8,128)(2,1)}, bf16[192,8,360]{2,0,1:T(8,128)(2,1)}, u32[]{:S(2)}, u32[]{:S(2)}) %collective-permute-start.4) | collective-permute-done | bytes 1105952 | tf_op jit(solution)/shard_map/ppermute | solution.py:92
  519.7 1.5 constant_dynamic-update-slice_fusion
  521.2 0.0 slice-done
  521.3 0.0 slice-done.1
  521.3 2.0 fusion.23
  523.3 5.0 copy.50
  (10 shorter events, 0.0 us)
Async XLA Ops:
  6.5 7.1 %copy-start.2 = (f32[9,192]{1,0:T(8,128)S(1)}, f32[9,192]{1,0:T(8,128)}, u32[]{:S(2)}) copy-start(f32[9,192]{1,0:T(8,128)} %param.7) | copy-start | bytes 20740
  6.5 241.4 %all-gather.3.cloned.1.call-start = ((), (), s32[]{:S(2)}) async-start(), calls=%async_computation.1 | async-start | bytes 5013504 | tf_op jit(solution)/shard_map/all_gather | solution.py:61
  10.4 11.0 %collective-permute-start = (bf16[192,32,8]{0,2,1:T(8,128)(2,1)S(1)}, bf16[192,32,8]{0,2,1:T(8,128)(2,1)S(1)}, u32[]{:S(2)}, u32[]{:S(2)}) collective-permute-start(bf16[192,32,8]{0,2,1:T(8,128)(2,1)S(1)} %copy.51), channel_id=1, source_target_pairs={{0,4},{4,8},{8,12},{12,0},{1,5},{5,9},{9,13},{13,1},{2,6},{6,10},{... | collective-permute-start | bytes 294920 | tf_op jit(solution)/shard_map/ppermute | solution.py:17
  11.8 10.4 %collective-permute-start.1 = (bf16[192,32,8]{0,2,1:T(8,128)(2,1)S(1)}, bf16[192,32,8]{0,2,1:T(8,128)(2,1)S(1)}, u32[]{:S(2)}, u32[]{:S(2)}) collective-permute-start(bf16[192,32,8]{0,2,1:T(8,128)(2,1)S(1)} %copy.52), channel_id=1, source_target_pairs={{4,0},{8,4},{12,8},{0,12},{5,1},{9,5},{13,9},{1,13},{6,2},{10,6},{... | collective-permute-start | bytes 294920 | tf_op jit(solution)/shard_map/ppermute | solution.py:18
  14.2 9.6 %copy-start.4 = (f32[1,192]{1,0:T(1,128)S(1)}, f32[1,192]{1,0:T(1,128)}, u32[]{:S(2)}) copy-start(f32[1,192]{1,0:T(1,128)} %get-tuple-element.28) | copy-start | bytes 2308
  67.5 135.2 %all-to-all-start = ((bf16[192,32,360]{2,0,1:T(8,128)(2,1)}), bf16[192,32,360]{2,0,1:T(8,128)(2,1)}, u32[]{:S(2)}, u32[]{:S(2)}) async-start(bf16[192,32,360]{2,0,1:T(8,128)(2,1)} %fusion.33), calls=%async_computation | async-start | bytes 9437184 | tf_op jit(solution)/shard_map/all_to_all | solution.py:57
  72.8 290.0 %all-gather.5.cloned.1.call-start = ((), (), s32[]{:S(2)}) async-start(), calls=%async_computation.2 | async-start | bytes 5013504 | tf_op jit(solution)/shard_map/all_gather | solution.py:67
  206.2 5.0 copy-start
  229.2 11.6 %copy-start.3 = (f32[768]{0:T(1024)S(1)}, f32[768]{0:T(1024)}, u32[]{:S(2)}) copy-start(f32[768]{0:T(1024)} %param.9) | copy-start | bytes 9220
  362.8 8.8 %copy-start.1 = (bf16[3072,2880]{1,0:T(8,128)(2,1)S(1)}, bf16[3072,2880]{1,0:T(8,128)(2,1)}, u32[]{:S(2)}) copy-start(bf16[3072,2880]{1,0:T(8,128)(2,1)} %copy.37) | copy-start | bytes 53084164
  362.8 10.8 %copy-start.5 = (bf16[768,3072]{0,1:T(8,128)(2,1)S(1)}, bf16[768,3072]{0,1:T(8,128)(2,1)}, u32[]{:S(2)}) copy-start(bf16[768,3072]{0,1:T(8,128)(2,1)} %all-gather.5.cloned.1.call-done) | copy-start | bytes 14155780
  411.2 49.8 %collective-permute-start.2 = (bf16[192,8,360]{2,0,1:T(8,128)(2,1)}, bf16[192,8,360]{2,0,1:T(8,128)(2,1)}, u32[]{:S(2)}, u32[]{:S(2)}) collective-permute-start(bf16[192,8,360]{2,0,1:T(8,128)(2,1)} %copy.62), channel_id=1, source_target_pairs={{0,1},{1,0},{2,3},{3,2},{4,5},{5,4},{6,7},{7,6},{8,9},{9,8},{10,11... | collective-permute-start | bytes 3317768 | tf_op jit(solution)/shard_map/ppermute | solution.py:92
  417.1 77.4 %collective-permute-start.3 = (bf16[192,8,360]{2,0,1:T(8,128)(2,1)}, bf16[192,8,360]{2,0,1:T(8,128)(2,1)}, u32[]{:S(2)}, u32[]{:S(2)}) collective-permute-start(bf16[192,8,360]{2,0,1:T(8,128)(2,1)} %copy.63), channel_id=1, source_target_pairs={{0,2},{1,3},{2,0},{3,1},{4,6},{5,7},{6,4},{7,5},{8,10},{9,11},{10,... | collective-permute-start | bytes 3317768 | tf_op jit(solution)/shard_map/ppermute | solution.py:92
  417.2 104.0 %slice-start = ((s8[4718592]{0:T(1024)(128)(4,1)}), s8[524288]{0:T(1024)(128)(4,1)S(1)}, s32[]{:S(2)}) async-start(s8[4718592]{0:T(1024)(128)(4,1)} %bitcast.174), calls=%async_computation.3 | async-start | bytes 1048576
  418.7 101.0 %collective-permute-start.4 = (bf16[192,8,360]{2,0,1:T(8,128)(2,1)}, bf16[192,8,360]{2,0,1:T(8,128)(2,1)}, u32[]{:S(2)}, u32[]{:S(2)}) collective-permute-start(bf16[192,8,360]{2,0,1:T(8,128)(2,1)} %copy.64), channel_id=1, source_target_pairs={{0,3},{1,2},{2,1},{3,0},{4,7},{5,6},{6,5},{7,4},{8,11},{9,10},{10,... | collective-permute-start | bytes 3317768 | tf_op jit(solution)/shard_map/ppermute | solution.py:92
  421.2 100.1 %slice-start.1 = ((s8[4718592]{0:T(1024)(128)(4,1)}), s8[4194304]{0:T(1024)(128)(4,1)S(1)}, s32[]{:S(2)}) async-start(s8[4718592]{0:T(1024)(128)(4,1)} %bitcast.174), calls=%async_computation.4 | async-start | bytes 8388608
Sparse Core Ops, SparseCore 0:
  13.7 54.5 all-gather.2
  86.0 111.4 all-gather.4
